TPU v7x, 32 devices: a whole 2x2x4 slice. The times are simulated.
32 devices in a mesh: dp: 16 (over z, y, core), ctx: 2 (over x).
Axes of the slice: x: 2, y: 2, z: 4, core: 2. Of those that a mesh axis runs over, the one named last changes fastest.
Arguments:
- conv_input: bfloat16 [16, 256, 4096], P('dp', 'ctx'), may hold values from -6 to 6
- gate_value: bfloat16 [16, 256, 4096], P('dp', 'ctx'), may hold values from -6 to 6
- out_grad: bfloat16 [16, 256, 4096], P('dp', 'ctx'), may hold values from -6 to 6
- filter_taps: bfloat16 [128, 4096], P('dp'), may hold values from -0.5 to 0.5
Outputs:
- input_grad: bfloat16 [16, 256, 4096], P('dp', 'ctx')
- filter_grad: float32 [128, 4096], P('dp')
All inputs are finite; a program needn't handle non-finite values.
Results may differ from a plain program's by a relative error of at most 0.0051.
Values may be sent and summed in bfloat16 or wider, within the bound.
A program may use at most 64 MiB of HBM per device.

v0:
```python
import math
import jax
import jax.numpy as jnp
import numpy as np
from jax import lax
from jax.sharding import PartitionSpec as P


def split(values):
    high = values.astype(jnp.bfloat16)
    return (high, (values - high.astype(np.float32)).astype(jnp.bfloat16))


def transforms(length):
    half = length // 2
    angle = np.pi * np.outer(2 * np.arange(half) + 1, np.arange(length)) / length
    forward = np.concatenate([np.cos(angle), -np.sin(angle)], 0)
    inverse = np.concatenate([np.cos(angle), -np.sin(angle)], 0).T / half
    return (split(forward.astype(np.float32)), split(inverse.astype(np.float32)))


def dot(a, b):
    return lax.dot_general(a, b, (((1,), (0,)), ((), ())), preferred_element_type=jnp.float32)


def shards(conv_input, gate_value, out_grad, filter_taps):
    inputs = conv_input[0]
    rows = inputs.shape[0]
    taps = filter_taps.shape[0] * lax.axis_size("dp")
    (fh, fl), (bh, bl) = transforms(rows + taps)
    half = (rows + taps) // 2
    mixed = (out_grad[0].astype(jnp.float32) * gate_value[0].astype(jnp.float32)).astype(
        jnp.bfloat16
    )
    devices = lax.axis_size("ctx")
    rim = lax.ppermute(mixed[:taps], "ctx", [(i + 1, i) for i in range(devices - 1)])
    full_taps = lax.all_gather(filter_taps, "dp", axis=0, tiled=True)

    def spectrum(x, first=0):
        n = x.shape[0]
        s = dot(fh[:, first : first + n], x) + dot(fl[:, first : first + n], x)
        return (s[:half], s[half:])

    def back(re, im, n):
        s = jnp.concatenate([re, im], 0)
        high = s.astype(jnp.bfloat16)
        low = (s - high.astype(jnp.float32)).astype(jnp.bfloat16)
        return dot(bh[:n], high) + dot(bl[:n], high) + dot(bh[:n], low)

    xr, xi = spectrum(inputs)
    gr0, gi0 = spectrum(mixed)
    gr1, gi1 = spectrum(rim, rows)
    gr, gi = (gr0 + gr1, gi0 + gi1)
    partial = back(xr * gr + xi * gi, xr * gi - xi * gr, taps)
    hr, hi = spectrum(full_taps)
    grad = back(hr * gr + hi * gi, hr * gi - hi * gr, rows)
    shard_grad = lax.psum(lax.psum_scatter(partial, "dp", scatter_dimension=0, tiled=True), "ctx")
    tokens_all = rows * devices * lax.axis_size("dp")
    return (grad.astype(jnp.bfloat16)[None], shard_grad * (1.0 / math.sqrt(tokens_all)))


def solution(mesh):
    in_specs = (P("dp", "ctx", None), P("dp", "ctx", None), P("dp", "ctx", None), P("dp", None))
    out_specs = (P("dp", "ctx", None), P("dp", None))
    return jax.shard_map(shards, mesh=mesh, in_specs=in_specs, out_specs=out_specs, check_vma=False)
```

profile of v0, /device:TPU:0, one launch (start us, length us, event | category | flops | bytes accessed | tf_op | source)
XLA Modules:
  0.0 203.6 jit_solution(12447030233872739120)
XLA Ops:
  7.2 0.0 copy-start
  7.2 0.0 copy-start.10
  7.2 0.0 all-gather.2.cloned.1.call-start
  7.2 1.9 fusion.7
  9.1 1.3 collective-permute-start
  10.4 0.0 all-gather.2.cloned.1.call-update
  10.4 0.0 reduce-scatter.4.cloned.1.call-start
  10.5 0.0 copy-done.10
  10.5 0.7 fusion.26
  11.2 0.0 copy-done
  11.2 0.0 copy-start.9
  11.2 0.7 fusion.9
  11.9 0.1 copy-done.9
  12.0 0.7 fusion.1
  12.8 0.0 copy-start.13
  12.8 0.7 convolution_add_fusion.2
  13.5 0.0 copy-start.2
  13.6 0.0 copy-start.12
  13.6 23.0 %collective-permute-done = bf16[128,4096]{1,0:T(8,128)(2,1)S(1)} collective-permute-done((bf16[128,4096]{1,0:T(8,128)(2,1)S(1)}, bf16[128,4096]{1,0:T(8,128)(2,1)S(1)}, u32[]{:S(2)}, u32[]{:S(2)}) %collective-permute-start) | collective-permute-done | bytes 1048608 | tf_op jit(solution)/shard_map/ppermute | solution.py:36
  36.6 0.0 copy-done.13
  36.6 0.7 fusion.27
  37.3 0.0 copy-done.12
  37.3 0.7 fusion
  38.0 0.0 copy-done.2
  38.0 3.2 %multiply_add_fusion = (f32[128,4096]{1,0:T(8,128)}, f32[128,4096]{1,0:T(8,128)}, f32[128,4096]{1,0:T(8,128)}) fusion(f32[256,4096]{1,0:T(8,128)S(1)} %convolution_add_fusion.2, f32[256,4096]{1,0:T(8,128)S(1)} %fusion, f32[256,4096]{1,0:T(8,128)S(1)} %fusion.1), kind=kLoop, calls=%fused_computation.22 | loop fusion | flops 2621440 | bytes 18874368 | tf_op jit(solution)/shard_map/add | solution.py:54
  41.2 11.2 %all-gather.2.cloned.1.call-done = bf16[128,4096]{1,0:T(8,128)(2,1)} async-done(((bf16[8,4096]{1,0:T(8,128)(2,1)}), bf16[128,4096]{1,0:T(8,128)(2,1)}) %all-gather.2.cloned.1.call-update) | async-done | bytes 1048592 | tf_op jit(solution)/shard_map/all_gather | solution.py:37
  52.4 0.0 copy-start.7
  52.4 2.0 fusion.25
  54.4 0.0 copy-done.7
  54.4 0.0 copy-start.3
  54.4 0.0 copy-start.6
  54.4 0.7 convolution_add_fusion.3
  55.2 1.4 copy-done.3
  56.6 0.7 copy-done.6
  57.3 0.0 copy-start.5
  57.3 0.0 copy-start.8
  57.3 4.2 %multiply_add_fusion.1 = (f32[128,4096]{1,0:T(8,128)S(1)}, f32[128,4096]{1,0:T(8,128)}, f32[128,4096]{1,0:T(8,128)S(1)}) fusion(f32[128,4096]{1,0:T(8,128)S(1)} %copy-done.6, f32[128,4096]{1,0:T(8,128)} %get-tuple-element.8, f32[256,4096]{1,0:T(8,128)S(1)} %convolution_add_fusion.3, f32[256,4096]{1,0:T(8,128)S(1)} %copy-done.3), kind=kLoop, calls=%fused_computation.24 | loop fusion | flops 4718592 | bytes 18874368 | tf_op jit(solution)/shard_map/add | solution.py:56
  61.5 0.0 copy-done.5
  61.5 0.0 copy-done.8
  61.5 0.0 copy-start.11
  61.5 0.8 fusion.17
  62.3 0.1 copy-done.11
  62.3 0.8 convolution_add_fusion.5
  63.1 2.1 %fusion.2 = f32[128,4096]{0,1:T(8,128)} fusion(f32[4096,128]{1,0:T(8,128)S(1)} %convolution_add_fusion.5, bf16[128,256]{1,0:T(8,128)(2,1)S(1)} %copy-done.8, f32[128,4096]{1,0:T(8,128)S(1)} %get-tuple-element.11, f32[128,4096]{1,0:T(8,128)S(1)} %copy-done.5), kind=kOutput, calls=%fused_computation.7 | convolution fusion | flops 274202624 | bytes 8454144 | tf_op jit(solution)/shard_map/dot_general | solution.py:23
  65.2 3.0 %copy.24 = f32[128,4096]{1,0:T(8,128)} copy(f32[128,4096]{0,1:T(8,128)} %fusion.2) | data formatting | bytes 4194304
  68.1 0.0 reduce-scatter.4.cloned.1.call-update
  68.2 0.2 all-reduce.2.cloned.1.call-start
  68.4 0.0 copy-start.4
  68.4 2.5 %fusion.13 = f32[4096,128]{1,0:T(8,128)S(1)} fusion(bf16[128,256]{1,0:T(8,128)(2,1)S(1)} %copy-done.8, f32[128,4096]{1,0:T(8,128)} %get-tuple-element.10, f32[128,4096]{1,0:T(8,128)S(1)} %get-tuple-element.9), kind=kOutput, calls=%fused_computation.31 | convolution fusion | flops 272629760 | bytes 6356992 | tf_op jit(solution)/shard_map/dot_general | solution.py:23
  70.9 0.0 copy-done.4
  70.9 2.1 %convolution_add_fusion.7 = f32[4096,128]{1,0:T(8,128)} fusion(f32[4096,128]{1,0:T(8,128)S(1)} %fusion.13, bf16[128,256]{1,0:T(8,128)(2,1)S(1)} %copy-done.11, f32[128,4096]{1,0:T(8,128)S(1)} %copy-done.4, f32[128,4096]{1,0:T(8,128)S(1)} %get-tuple-element.9), kind=kOutput, calls=%fused_computation.10 | convolution fusion | flops 273154048 | bytes 8454144 | tf_op jit(solution)/shard_map/dot_general | solution.py:23
  73.0 56.1 %reduce-scatter.4.cloned.1.call-done = f32[8,4096]{1,0:T(8,128)} async-done(((f32[128,4096]{1,0:T(8,128)}), f32[8,4096]{1,0:T(8,128)}) %reduce-scatter.4.cloned.1.call-update) | async-done | bytes 131088
  129.1 2.9 %copy.25 = f32[8,4096]{0,1:T(8,128)} copy(f32[8,4096]{1,0:T(8,128)} %reduce-scatter.4.cloned.1.call-done) | data formatting | bytes 262144
  132.0 0.0 all-reduce.2.cloned.1.call-update
  132.0 3.0 %fusion.4 = bf16[1,128,4096]{1,2,0:T(8,128)(2,1)S(1)} fusion(f32[4096,128]{1,0:T(8,128)} %convolution_add_fusion.7, bf16[128,256]{1,0:T(8,128)(2,1)S(1)} %copy-done.8, f32[128,4096]{1,0:T(8,128)} %get-tuple-element.10, f32[128,4096]{1,0:T(8,128)S(1)} %get-tuple-element.9), kind=kOutput, calls=%fused_computation.12 | convolution fusion | flops 274726912 | bytes 7405568 | tf_op jit(solution)/shard_map/dot_general | solution.py:23
  135.0 1.3 copy.22
  136.3 57.7 %all-reduce.2.cloned.1.call-done = f32[8,4096]{0,1:T(8,128)} async-done(((f32[8,4096]{0,1:T(8,128)}), f32[8,4096]{0,1:T(8,128)}) %all-reduce.2.cloned.1.call-update) | async-done | bytes 131088 | tf_op jit(solution)/shard_map/psum | solution.py:57
  194.0 0.0 copy-start.1
  194.0 1.8 broadcast_multiply_fusion
  195.8 1.2 copy.23
  197.1 0.0 copy-done.1
Async XLA Ops:
  7.2 4.0 %copy-start = (bf16[1,128,4096]{2,1,0:T(8,128)(2,1)S(1)}, bf16[1,128,4096]{2,1,0:T(8,128)(2,1)}, u32[]{:S(2)}) copy-start(bf16[1,128,4096]{2,1,0:T(8,128)(2,1)} %param.18) | copy-start | bytes 3145732
  7.2 3.3 %copy-start.10 = (bf16[256,128]{1,0:T(8,128)(2,1)S(1)}, bf16[256,128]{1,0:T(8,128)(2,1)}, u32[]{:S(2)}) copy-start(bf16[256,128]{1,0:T(8,128)(2,1)} %constant.14.clone) | copy-start | bytes 196612
  7.2 45.2 %all-gather.2.cloned.1.call-start = ((), (), s32[]{:S(2)}) async-start(), calls=%async_computation.1 | async-start | bytes 1114112 | tf_op jit(solution)/shard_map/all_gather | solution.py:37
  9.1 27.5 %collective-permute-start = (bf16[128,4096]{1,0:T(8,128)(2,1)S(1)}, bf16[128,4096]{1,0:T(8,128)(2,1)S(1)}, u32[]{:S(2)}, u32[]{:S(2)}) collective-permute-start(bf16[128,4096]{1,0:T(8,128)(2,1)S(1)} %fusion.7), channel_id=1, source_target_pairs={{1,0},{3,2},{5,4},{7,6},{9,8},{11,10},{13,12},{15,14},{17,16},{19,... | collective-permute-start | bytes 3145736 | tf_op jit(solution)/shard_map/ppermute | solution.py:36
  10.4 118.7 %reduce-scatter.4.cloned.1.call-start = ((), (), s32[]{:S(2)}) async-start(), calls=%async_computation.3 | async-start | bytes 2228224
  11.2 0.8 copy-start.9
  12.8 23.8 %copy-start.13 = (bf16[256,128]{1,0:T(8,128)(2,1)S(1)}, bf16[256,128]{1,0:T(8,128)(2,1)}, u32[]{:S(2)}) copy-start(bf16[256,128]{1,0:T(8,128)(2,1)} %constant.17.clone) | copy-start | bytes 196612
  13.5 24.5 %copy-start.2 = (f32[256,4096]{1,0:T(8,128)}, f32[256,4096]{1,0:T(8,128)S(1)}, u32[]{:S(2)}) copy-start(f32[256,4096]{1,0:T(8,128)S(1)} %convolution_add_fusion.2) | copy-start | bytes 12582916
  13.6 23.7 %copy-start.12 = (bf16[256,128]{1,0:T(8,128)(2,1)S(1)}, bf16[256,128]{1,0:T(8,128)(2,1)}, u32[]{:S(2)}) copy-start(bf16[256,128]{1,0:T(8,128)(2,1)} %constant.16.clone) | copy-start | bytes 196612
  52.4 2.0 copy-start.7
  54.4 2.2 %copy-start.3 = (f32[256,4096]{1,0:T(8,128)S(1)}, f32[256,4096]{1,0:T(8,128)}, u32[]{:S(2)}) copy-start(f32[256,4096]{1,0:T(8,128)} %copy-done.2) | copy-start | bytes 12582916
  54.4 2.9 %copy-start.6 = (f32[128,4096]{1,0:T(8,128)S(1)}, f32[128,4096]{1,0:T(8,128)}, u32[]{:S(2)}) copy-start(f32[128,4096]{1,0:T(8,128)} %get-tuple-element.7) | copy-start | bytes 6291460
  57.3 4.2 %copy-start.5 = (f32[128,4096]{1,0:T(8,128)S(1)}, f32[128,4096]{1,0:T(8,128)}, u32[]{:S(2)}) copy-start(f32[128,4096]{1,0:T(8,128)} %get-tuple-element.6) | copy-start | bytes 6291460
  57.3 4.2 %copy-start.8 = (bf16[128,256]{1,0:T(8,128)(2,1)S(1)}, bf16[128,256]{1,0:T(8,128)(2,1)}, u32[]{:S(2)}) copy-start(bf16[128,256]{1,0:T(8,128)(2,1)} %constant.18.clone) | copy-start | bytes 196612
  61.5 0.8 copy-start.11
  68.2 125.9 %all-reduce.2.cloned.1.call-start = ((), (), s32[]{:S(2)}) async-start(), calls=%async_computation.2 | async-start | bytes 4194304 | tf_op jit(solution)/shard_map/psum | solution.py:57
  68.4 2.5 %copy-start.4 = (f32[128,4096]{1,0:T(8,128)S(1)}, f32[128,4096]{1,0:T(8,128)}, u32[]{:S(2)}) copy-start(f32[128,4096]{1,0:T(8,128)} %get-tuple-element.10) | copy-start | bytes 6291460
  194.0 3.1 %copy-start.1 = (bf16[1,128,4096]{2,1,0:T(8,128)(2,1)S(1)}, bf16[1,128,4096]{2,1,0:T(8,128)(2,1)}, u32[]{:S(2)}) copy-start(bf16[1,128,4096]{2,1,0:T(8,128)(2,1)} %param.18) | copy-start | bytes 3145732
Sparse Core Ops, SparseCore 0:
  10.6 41.7 all-gather.1
  68.3 60.7 reduce-scatter.3
  132.1 61.8 all-reduce.1
where the time goes:
time: 204 us
  waiting for transfers between devices  148 us (73%)
  matrix products  18.2 us (9%)
  between operations  14 us (7%)
  other arithmetic  11.1 us (5%)
  local copies, waits for them, and re-layouts  10.7 us (5%)
    psum x1, waiting for transfers between devices, shards(): lax.psum(lax.psum_scatter(partial, 'dp', scatter_dimension=0, tiled=True)...  57.7 us
    unnamed x4, waiting for transfers between devices  56.1 us
    ppermute x1, waiting for transfers between devices, shards(): lax.ppermute(mixed[:taps], 'ctx', [(i + 1, i) for i in range(devices - 1)])  23 us
    dot_general x14, matrix products, dot(): lax.dot_general(a, b, (((1,), (0,)), ((), ())), preferred_element_type=jn...  18.2 us
    all_gather x1, waiting for transfers between devices, shards(): full_taps = lax.all_gather(filter_taps, 'dp', axis=0, tiled=True)  11.2 us
    unnamed x32, local copies, waits for them, and re-layouts  10.7 us
    add x1, other arithmetic, shards(): grad = back(hr * gr + hi * gi, hr * gi - hi * gr, rows)  4.21 us
  transfers between devices with their start and end apart: 4, of which 4 were waited for; matrix products, arithmetic and copies ran while one was open for 8% of the time, Pallas kernels for 0%

commit v1 on v0

--- a/solution.py
+++ b/solution.py
@@ -1,9 +1,18 @@
+import functools
 import math
 import jax
 import jax.numpy as jnp
 import numpy as np
 from jax import lax
 from jax.sharding import PartitionSpec as P
+
+
+def place_the_sheet(payload, a_name):
+    local_next = lax.all_gather(payload, a_name).sum(axis=0)
+    return local_next
+
+
+fill_pages_in = functools.partial(place_the_sheet, a_name="ctx")
 
 
 def split(values):
@@ -54,7 +63,7 @@
     partial = back(xr * gr + xi * gi, xr * gi - xi * gr, taps)
     hr, hi = spectrum(full_taps)
     grad = back(hr * gr + hi * gi, hr * gi - hi * gr, rows)
-    shard_grad = lax.psum(lax.psum_scatter(partial, "dp", scatter_dimension=0, tiled=True), "ctx")
+    shard_grad = fill_pages_in(lax.psum_scatter(partial, "dp", scatter_dimension=0, tiled=True))
     tokens_all = rows * devices * lax.axis_size("dp")
     return (grad.astype(jnp.bfloat16)[None], shard_grad * (1.0 / math.sqrt(tokens_all)))
 

time: 204 us -> 143 us (0.70)
  waiting for transfers between devices: 148 us -> 87.7 us
  blocking collectives: 0 us -> 5.83 us
  local copies, waits for them, and re-layouts: 10.7 us -> 7.59 us
  matrix products: 18.2 us -> 15.7 us
    psum x1 -> x0, waiting for transfers between devices: 57.7 us -> none  [shards(): lax.psum(lax.psum_scatter(partial, 'dp', scatter_dimension=0, tiled=True)...]
    unnamed x4 -> x2, waiting for transfers between devices: 56.1 us -> 0.03 us
    reduce_scatter x0 -> x1, waiting for transfers between devices: none -> 53.6 us  [shards(): lax.psum_scatter(partial, 'dp', scatter_dimension=0, tiled=True)]
    all_gather x0 -> x1, blocking collectives: none -> 5.83 us  [place_the_sheet(): local_next = lax.all_gather(payload, a_name).sum(axis=0)]
    unnamed x32 -> x30, local copies, waits for them, and re-layouts: 10.7 us -> 7.59 us
    dot_general x14, matrix products: 18.2 us -> 15.7 us  [dot(): lax.dot_general(a, b, (((1,), (0,)), ((), ())), preferred_element_type=jn...]
  transfers between devices with their start and end apart: 4 -> 3, of which waited for: 4 -> 3; matrix products, arithmetic and copies ran while one was open for 8% -> 10% of each run, Pallas kernels for 0% -> 0%
where the time goes in v1:
time: 143 us; the launch traced here: 142 us
  waiting for transfers between devices  87.7 us (61%)
  matrix products  15.7 us (11%)
  between operations  14.3 us (10%)
  other arithmetic  9.98 us (7%)
  local copies, waits for them, and re-layouts  7.59 us (5%)
  blocking collectives  5.83 us (4%)
    reduce_scatter x1, waiting for transfers between devices, shards(): lax.psum_scatter(partial, 'dp', scatter_dimension=0, tiled=True)  53.6 us
    ppermute x1, waiting for transfers between devices, shards(): lax.ppermute(mixed[:taps], 'ctx', [(i + 1, i) for i in range(devices - 1)])  23 us
    dot_general x14, matrix products, dot(): lax.dot_general(a, b, (((1,), (0,)), ((), ())), preferred_element_type=jn...  15.7 us
    all_gather x1, waiting for transfers between devices, shards(): full_taps = lax.all_gather(filter_taps, 'dp', axis=0, tiled=True)  11.1 us
    unnamed x30, local copies, waits for them, and re-layouts  7.59 us
    all_gather x1, blocking collectives, place_the_sheet(): local_next = lax.all_gather(payload, a_name).sum(axis=0)  5.83 us
    add x1, other arithmetic, shards(): grad = back(hr * gr + hi * gi, hr * gi - hi * gr, rows)  4.21 us
    add x1, other arithmetic, shards(): partial = back(xr * gr + xi * gi, xr * gi - xi * gr, taps)  3.22 us
  transfers between devices with their start and end apart: 3, of which 3 were waited for; matrix products, arithmetic and copies ran while one was open for 10% of the time, Pallas kernels for 0%

profile of v1, /device:TPU:0, one launch (start us, length us, event | category | flops | bytes accessed | tf_op | source)
XLA Modules:
  0.0 142.5 jit_solution(1577224262711718549)
XLA Ops:
  7.2 0.0 copy-start
  7.2 0.0 copy-start.10
  7.2 0.0 all-gather.3.cloned.1.call-start
  7.2 1.9 %fusion.7 = bf16[128,4096]{1,0:T(8,128)(2,1)S(1)} fusion(bf16[1,128,4096]{2,1,0:T(8,128)(2,1)} %param.19, bf16[1,128,4096]{2,1,0:T(8,128)(2,1)} %param.20), kind=kLoop, calls=%fused_computation.26 | loop fusion | flops 2097152 | bytes 3145728 | tf_op jit(solution)/shard_map/convert_element_type | solution.py:41
  9.1 1.3 collective-permute-start
  10.4 0.0 all-gather.3.cloned.1.call-update
  10.4 0.0 reduce-scatter.4.cloned.1.call-start
  10.5 0.0 copy-done.10
  10.5 0.7 fusion.26
  11.2 0.0 copy-done
  11.2 0.0 copy-start.9
  11.2 0.7 fusion.9
  11.9 0.1 copy-done.9
  12.0 0.7 fusion.1
  12.8 0.0 copy-start.13
  12.8 0.7 convolution_add_fusion.2
  13.5 0.0 copy-start.2
  13.6 0.0 copy-start.12
  13.6 23.0 %collective-permute-done = bf16[128,4096]{1,0:T(8,128)(2,1)S(1)} collective-permute-done((bf16[128,4096]{1,0:T(8,128)(2,1)S(1)}, bf16[128,4096]{1,0:T(8,128)(2,1)S(1)}, u32[]{:S(2)}, u32[]{:S(2)}) %collective-permute-start) | collective-permute-done | bytes 1048608 | tf_op jit(solution)/shard_map/ppermute | solution.py:45
  36.6 0.0 copy-done.13
  36.6 0.7 fusion.27
  37.3 0.0 copy-done.12
  37.3 0.7 fusion
  38.0 0.0 copy-done.2
  38.0 3.2 %multiply_add_fusion = (f32[128,4096]{1,0:T(8,128)}, f32[128,4096]{1,0:T(8,128)}, f32[128,4096]{1,0:T(8,128)}) fusion(f32[256,4096]{1,0:T(8,128)S(1)} %convolution_add_fusion.2, f32[256,4096]{1,0:T(8,128)S(1)} %fusion, f32[256,4096]{1,0:T(8,128)S(1)} %fusion.1), kind=kLoop, calls=%fused_computation.22 | loop fusion | flops 2621440 | bytes 18874368 | tf_op jit(solution)/shard_map/add | solution.py:63
  41.2 11.1 %all-gather.3.cloned.1.call-done = bf16[128,4096]{1,0:T(8,128)(2,1)} async-done(((bf16[8,4096]{1,0:T(8,128)(2,1)}), bf16[128,4096]{1,0:T(8,128)(2,1)}) %all-gather.3.cloned.1.call-update) | async-done | bytes 1048592 | tf_op jit(solution)/shard_map/all_gather | solution.py:46
  52.4 0.0 copy-start.7
  52.4 2.0 %fusion.25 = f32[256,4096]{1,0:T(8,128)S(1)} fusion(bf16[256,128]{1,0:T(8,128)(2,1)S(1)} %copy-done.10, bf16[128,4096]{1,0:T(8,128)(2,1)} %all-gather.3.cloned.1.call-done), kind=kOutput, calls=%fused_computation.40 | convolution fusion | flops 268435456 | bytes 5308416 | tf_op jit(solution)/shard_map/dot_general | solution.py:32
  54.4 0.0 copy-done.7
  54.4 0.0 copy-start.3
  54.4 0.0 copy-start.6
  54.4 0.7 convolution_add_fusion.3
  55.2 1.4 %copy-done.3 = f32[256,4096]{1,0:T(8,128)S(1)} copy-done((f32[256,4096]{1,0:T(8,128)S(1)}, f32[256,4096]{1,0:T(8,128)}, u32[]{:S(2)}) %copy-start.3) | copy-done | bytes 4194328
  56.6 0.7 copy-done.6
  57.3 0.0 copy-start.5
  57.3 0.0 copy-start.8
  57.3 4.2 %multiply_add_fusion.1 = (f32[128,4096]{1,0:T(8,128)S(1)}, f32[128,4096]{1,0:T(8,128)}, f32[128,4096]{1,0:T(8,128)S(1)}) fusion(f32[128,4096]{1,0:T(8,128)S(1)} %copy-done.6, f32[128,4096]{1,0:T(8,128)} %get-tuple-element.10, f32[256,4096]{1,0:T(8,128)S(1)} %convolution_add_fusion.3, f32[256,4096]{1,0:T(8,128)S(1)} %copy-done.3), kind=kLoop, calls=%fused_computation.24 | loop fusion | flops 4718592 | bytes 18874368 | tf_op jit(solution)/shard_map/add | solution.py:65
  61.5 0.0 copy-done.5
  61.5 0.0 copy-done.8
  61.5 0.0 copy-start.11
  61.5 0.8 fusion.17
  62.3 0.1 copy-done.11
  62.3 0.8 convolution_add_fusion.5
  63.1 2.1 %fusion.2 = f32[128,4096]{0,1:T(8,128)} fusion(f32[4096,128]{1,0:T(8,128)S(1)} %convolution_add_fusion.5, bf16[128,256]{1,0:T(8,128)(2,1)S(1)} %copy-done.8, f32[128,4096]{1,0:T(8,128)S(1)} %get-tuple-element.13, f32[128,4096]{1,0:T(8,128)S(1)} %copy-done.5), kind=kOutput, calls=%fused_computation.7 | convolution fusion | flops 274202624 | bytes 8454144 | tf_op jit(solution)/shard_map/dot_general | solution.py:32
  65.2 2.9 %copy.25 = f32[128,4096]{1,0:T(8,128)} copy(f32[128,4096]{0,1:T(8,128)} %fusion.2) | data formatting | bytes 4194304
  68.2 0.0 reduce-scatter.4.cloned.1.call-update
  68.2 0.0 copy-start.4
  68.2 2.5 %fusion.13 = f32[4096,128]{1,0:T(8,128)S(1)} fusion(bf16[128,256]{1,0:T(8,128)(2,1)S(1)} %copy-done.8, f32[128,4096]{1,0:T(8,128)} %get-tuple-element.12, f32[128,4096]{1,0:T(8,128)S(1)} %get-tuple-element.11), kind=kOutput, calls=%fused_computation.30 | convolution fusion | flops 272629760 | bytes 6356992 | tf_op jit(solution)/shard_map/dot_general | solution.py:32
  70.7 0.0 copy-done.4
  70.7 0.8 convolution_add_fusion.7
  71.5 0.0 copy-start.1
  71.5 1.8 %fusion.4 = bf16[1,128,4096]{1,2,0:T(8,128)(2,1)} fusion(f32[4096,128]{1,0:T(8,128)S(1)} %convolution_add_fusion.7, bf16[128,256]{1,0:T(8,128)(2,1)S(1)} %copy-done.8, f32[128,4096]{1,0:T(8,128)S(1)} %copy-done.4, f32[128,4096]{1,0:T(8,128)S(1)} %get-tuple-element.11), kind=kOutput, calls=%fused_computation.12 | convolution fusion | flops 274726912 | bytes 7405568 | tf_op jit(solution)/shard_map/dot_general | solution.py:32
  73.3 2.3 %copy.24 = bf16[1,128,4096]{2,1,0:T(8,128)(2,1)} copy(bf16[1,128,4096]{1,2,0:T(8,128)(2,1)} %fusion.4) | data formatting | bytes 2097152
  75.6 53.6 %reduce-scatter.4.cloned.1.call-done = f32[8,4096]{1,0:T(8,128)} async-done(((f32[128,4096]{1,0:T(8,128)}), f32[8,4096]{1,0:T(8,128)}) %reduce-scatter.4.cloned.1.call-update) | async-done | bytes 131088 | tf_op jit(solution)/shard_map/reduce_scatter | solution.py:66
  129.1 5.8 %all-gather = f32[16,4096]{1,0:T(8,128)S(1)} all-gather(f32[8,4096]{1,0:T(8,128)} %reduce-scatter.4.cloned.1.call-done), channel_id=2, replica_groups=mesh['dp'=16,'ctx'=2] {'ctx'}, dimensions={0}, use_global_device_ids=true | all-gather | bytes 393216 | tf_op jit(solution)/shard_map/all_gather | solution.py:11
  135.0 0.7 broadcast_multiply_fusion
  135.6 0.0 copy-done.1
  (1 shorter events, 0.0 us)
Async XLA Ops:
  7.2 4.0 %copy-start = (bf16[1,128,4096]{2,1,0:T(8,128)(2,1)S(1)}, bf16[1,128,4096]{2,1,0:T(8,128)(2,1)}, u32[]{:S(2)}) copy-start(bf16[1,128,4096]{2,1,0:T(8,128)(2,1)} %param.18) | copy-start | bytes 3145732
  7.2 3.3 %copy-start.10 = (bf16[256,128]{1,0:T(8,128)(2,1)S(1)}, bf16[256,128]{1,0:T(8,128)(2,1)}, u32[]{:S(2)}) copy-start(bf16[256,128]{1,0:T(8,128)(2,1)} %constant.16.clone) | copy-start | bytes 196612
  7.2 45.2 %all-gather.3.cloned.1.call-start = ((), (), s32[]{:S(2)}) async-start(), calls=%async_computation.1 | async-start | bytes 1114112 | tf_op jit(solution)/shard_map/all_gather | solution.py:46
  9.1 27.5 %collective-permute-start = (bf16[128,4096]{1,0:T(8,128)(2,1)S(1)}, bf16[128,4096]{1,0:T(8,128)(2,1)S(1)}, u32[]{:S(2)}, u32[]{:S(2)}) collective-permute-start(bf16[128,4096]{1,0:T(8,128)(2,1)S(1)} %fusion.7), channel_id=1, source_target_pairs={{1,0},{3,2},{5,4},{7,6},{9,8},{11,10},{13,12},{15,14},{17,16},{19,... | collective-permute-start | bytes 3145736 | tf_op jit(solution)/shard_map/ppermute | solution.py:45
  10.4 118.7 %reduce-scatter.4.cloned.1.call-start = ((), (), s32[]{:S(2)}) async-start(), calls=%async_computation.2 | async-start | bytes 2228224 | tf_op jit(solution)/shard_map/reduce_scatter | solution.py:66
  11.2 0.8 copy-start.9
  12.8 23.8 %copy-start.13 = (bf16[256,128]{1,0:T(8,128)(2,1)S(1)}, bf16[256,128]{1,0:T(8,128)(2,1)}, u32[]{:S(2)}) copy-start(bf16[256,128]{1,0:T(8,128)(2,1)} %constant.19.clone) | copy-start | bytes 196612
  13.5 24.5 %copy-start.2 = (f32[256,4096]{1,0:T(8,128)}, f32[256,4096]{1,0:T(8,128)S(1)}, u32[]{:S(2)}) copy-start(f32[256,4096]{1,0:T(8,128)S(1)} %convolution_add_fusion.2) | copy-start | bytes 12582916
  13.6 23.7 %copy-start.12 = (bf16[256,128]{1,0:T(8,128)(2,1)S(1)}, bf16[256,128]{1,0:T(8,128)(2,1)}, u32[]{:S(2)}) copy-start(bf16[256,128]{1,0:T(8,128)(2,1)} %constant.18.clone) | copy-start | bytes 196612
  52.4 2.0 %copy-start.7 = (bf16[128,4096]{1,0:T(8,128)(2,1)S(1)}, bf16[128,4096]{1,0:T(8,128)(2,1)}, u32[]{:S(2)}) copy-start(bf16[128,4096]{1,0:T(8,128)(2,1)} %all-gather.3.cloned.1.call-done) | copy-start | bytes 3145732
  54.4 2.2 %copy-start.3 = (f32[256,4096]{1,0:T(8,128)S(1)}, f32[256,4096]{1,0:T(8,128)}, u32[]{:S(2)}) copy-start(f32[256,4096]{1,0:T(8,128)} %copy-done.2) | copy-start | bytes 12582916
  54.4 2.9 %copy-start.6 = (f32[128,4096]{1,0:T(8,128)S(1)}, f32[128,4096]{1,0:T(8,128)}, u32[]{:S(2)}) copy-start(f32[128,4096]{1,0:T(8,128)} %get-tuple-element.9) | copy-start | bytes 6291460
  57.3 4.2 %copy-start.5 = (f32[128,4096]{1,0:T(8,128)S(1)}, f32[128,4096]{1,0:T(8,128)}, u32[]{:S(2)}) copy-start(f32[128,4096]{1,0:T(8,128)} %get-tuple-element.8) | copy-start | bytes 6291460
  57.3 4.2 %copy-start.8 = (bf16[128,256]{1,0:T(8,128)(2,1)S(1)}, bf16[128,256]{1,0:T(8,128)(2,1)}, u32[]{:S(2)}) copy-start(bf16[128,256]{1,0:T(8,128)(2,1)} %constant.20.clone) | copy-start | bytes 196612
  61.5 0.8 copy-start.11
  68.2 2.5 %copy-start.4 = (f32[128,4096]{1,0:T(8,128)S(1)}, f32[128,4096]{1,0:T(8,128)}, u32[]{:S(2)}) copy-start(f32[128,4096]{1,0:T(8,128)} %get-tuple-element.12) | copy-start | bytes 6291460
  71.5 64.1 %copy-start.1 = (bf16[1,128,4096]{2,1,0:T(8,128)(2,1)S(1)}, bf16[1,128,4096]{2,1,0:T(8,128)(2,1)}, u32[]{:S(2)}) copy-start(bf16[1,128,4096]{2,1,0:T(8,128)(2,1)} %param.18) | copy-start | bytes 3145732
Sparse Core Ops, SparseCore 0:
  10.6 41.7 all-gather.2
  68.3 60.7 reduce-scatter.3
